TPU v7x, 32 devices: a whole 2x2x4 slice. The times are simulated.
32 devices in a mesh: grp: 2 (over x), src: 8 (over z, y), tgt: 2 (over core).
Axes of the slice: x: 2, y: 2, z: 4, core: 2. Of those that a mesh axis runs over, the one named last changes fastest.
Arguments:
- densities: bfloat16 [512, 32768], P('grp', ('src', 'tgt')), parts along dimension 0, may hold values from -6 to 6
- compress: bfloat16 [65536, 2, 256], P(('grp', 'src', 'tgt')), parts along dimension 0, may hold values from -0.0625 to 0.0625
- level_a: bfloat16 [6, 2048, 2, 256], P('grp', 'src', None, 'tgt'), parts along dimension 0, may hold values from -0.1875 to 0.1875
- level_b: bfloat16 [6, 2048, 2, 256], P('grp', 'src', None, 'tgt'), parts along dimension 0, may hold values from -0.1875 to 0.1875
- expand: bfloat16 [4096, 2, 4096], P(('grp', 'src'), None, 'tgt'), parts along dimension 0, may hold values from -0.25 to 0.25
- near_tiles: bfloat16 [2048, 128, 2, 128], P(('grp', 'src', 'tgt')), parts along dimension 0, may hold values from -0.375 to 0.375
- tile_pairs: int32 [2048, 2], P(('grp', 'src', 'tgt')), parts along dimension 0, may hold values from 0 to 15
- tile_count: int32 [32], P(('grp', 'src', 'tgt')), parts along dimension 0, may hold values from 1 to 63, as said below
- cluster_order: int32 [32, 16], P(('grp', 'src', 'tgt')), parts along dimension 0, may hold values from 0 to 15, each once within a row
Outputs:
- potential: bfloat16 [512, 32768], P('grp', ('src', 'tgt')), parts along dimension 0
There are 2 independent parts, one for each index of `grp`. A program takes and returns all parts, laid end to end along the dimension named above; each array names one. Nothing has to cross between parts.
Inputs may be any that keep to these rules, and one draw needn't show every extreme that they name: For every i below 8, tile_count[i] + tile_count[i + 8] == 64; slots at or beyond a device's count are unused. `cluster_order`: each row is a permutation.
All inputs are finite; a program needn't handle non-finite values.
Results may differ from a plain program's by a relative error of at most 0.007.
Values may be sent and summed in bfloat16 or wider, within the bound.
No kernel may reach another device: no remote copies, remote signals or barrier semaphores. Data moves between devices by JAX's collectives and lax.ppermute only.
A program may use at most 128 MiB of HBM per device.

v0:
```python
import functools

import jax
import jax.numpy as jnp
from jax import lax
from jax.experimental import pallas as pl
from jax.experimental.pallas import tpu as pltpu
from jax.sharding import PartitionSpec as P


EXPAND_CHUNKS = 4
UNROLL = 16


def in_vmem():
    return pl.BlockSpec(memory_space=pltpu.VMEM)


def in_smem():
    return pl.BlockSpec(memory_space=pltpu.SMEM)


def in_hbm():
    return pl.BlockSpec(memory_space=pltpu.HBM)


def swapped(value, axis, bit):
    mask = 2**bit
    pairs = [(source, source ^ mask) for source in range(lax.axis_size(axis))]
    return lax.ppermute(value, axis, pairs)


def paired(block):
    half = block.shape[0] // 2
    upper, lower = block[:half], block[half:]
    return jnp.concatenate(
        [jnp.concatenate([upper, -lower], axis=1), jnp.concatenate([lower, upper], axis=1)], axis=0
    )


def first_kernel(dens_ref, mixed_ref, total, weave):
    clusters = mixed_ref.shape[0]
    width = dens_ref.shape[1] // clusters
    row_id = lax.broadcasted_iota(jnp.int32, weave.shape, 0)
    col_id = lax.broadcasted_iota(jnp.int32, weave.shape, 1)
    goal = jnp.where(row_id < width, 2 * row_id, 2 * (row_id - width) + 1)
    weave[...] = jnp.where(col_id == goal, 1.0, 0.0).astype(jnp.bfloat16)
    for cluster in range(clusters):
        block = paired(dens_ref[:, cluster * width : (cluster + 1) * width])
        woven = jnp.dot(block, weave[...], preferred_element_type=jnp.float32)
        mixed_ref[cluster] = woven.astype(jnp.bfloat16)
    total[...] = jnp.zeros_like(total)


def tiles_kernel(first, last, table_ref, count_ref, mixed_ref, tiles_ref, before, total):
    clusters = mixed_ref.shape[0]
    width = tiles_ref.shape[2]
    count = count_ref[0]
    for start in range(first, last, UNROLL):

        @pl.when(start < count)
        def _():
            table = table_ref[...]
            for slot in range(start, min(start + UNROLL, last)):
                target = jnp.where(slot < count, table[0, slot], clusters)
                columns = pl.ds(pl.multiple_of(target * width, width), width)
                total[:, columns] += jnp.dot(
                    mixed_ref[table[1, slot]], tiles_ref[slot], preferred_element_type=jnp.float32
                )


def first_call(densities, clusters):
    rows, points = densities.shape
    width = points // clusters
    return pl.pallas_call(
        first_kernel,
        out_shape=(
            jax.ShapeDtypeStruct((clusters, rows, 2 * width), jnp.bfloat16),
            jax.ShapeDtypeStruct((rows, points + width), jnp.float32),
        ),
        in_specs=[in_vmem()],
        out_specs=(in_vmem(), in_vmem()),
        scratch_shapes=[pltpu.VMEM((2 * width, 2 * width), jnp.bfloat16)],
        cost_estimate=pl.CostEstimate(
            flops=4 * rows * points * width, bytes_accessed=0, transcendentals=0
        ),
        compiler_params=pltpu.CompilerParams(vmem_limit_bytes=16 << 20),
        name="weave",
    )(densities)


def tiles_call(first, last, table, count, mixed, tiles, total):
    depth, width = tiles.shape[1:]
    return pl.pallas_call(
        functools.partial(tiles_kernel, first, last),
        out_shape=jax.ShapeDtypeStruct(total.shape, total.dtype),
        in_specs=[in_vmem(), in_smem(), in_vmem(), in_vmem(), in_vmem()],
        out_specs=in_vmem(),
        input_output_aliases={4: 0},
        cost_estimate=pl.CostEstimate(
            flops=2 * total.shape[0] * depth * width * (last - first),
            bytes_accessed=0,
            transcendentals=0,
        ),
        compiler_params=pltpu.CompilerParams(vmem_limit_bytes=16 << 20),
        name="tiles",
    )(table, count, mixed, tiles, total)


def far_rows(half, coeff_ref, matrix_ref, near_ref, rows_ref, columns):
    quarter = near_ref.shape[0] // 4
    far = jnp.dot(
        paired(coeff_ref[...]), matrix_ref[:, columns], preferred_element_type=jnp.float32
    )
    for part in range(2):
        source = pl.ds(pl.multiple_of((2 * part + half) * quarter, quarter), quarter)
        inner = slice(part * quarter, (part + 1) * quarter)
        rows_ref[inner, columns] = (far[inner] + near_ref[source, columns]).astype(jnp.bfloat16)


def expand_kernel(flip, order_ref, coeff_ref, matrix_ref, near_ref, *refs):
    out_hbm, rows_ref, sem = refs[-3:]
    quarter = near_ref.shape[0] // 4
    points = matrix_ref.shape[1]
    clusters = order_ref.shape[1]
    width = points // clusters
    core = lax.axis_index("tgt")
    half = 1 - core if flip else core
    order = order_ref[...]
    span = points // EXPAND_CHUNKS
    for chunk in range(EXPAND_CHUNKS):
        columns = slice(chunk * span, (chunk + 1) * span)
        far_rows(half, coeff_ref, matrix_ref, near_ref, rows_ref, columns)
        for cluster in range(
            chunk * clusters // EXPAND_CHUNKS, (chunk + 1) * clusters // EXPAND_CHUNKS
        ):
            place = pl.multiple_of(order[0, cluster] * width, width)
            source = slice(cluster * width, (cluster + 1) * width)
            for part in range(2):
                target = pl.ds(pl.multiple_of((2 * part + half) * quarter, quarter), quarter)
                pltpu.make_async_copy(
                    rows_ref.at[part * quarter : (part + 1) * quarter, source],
                    out_hbm.at[target, pl.ds(place, width)],
                    sem.at[0],
                ).start()
    pltpu.make_async_copy(rows_ref, out_hbm.at[0 : 2 * quarter, :], sem.at[0]).wait()


def expand_call(flip, order, coefficients, matrix, near, result):
    rows = near.shape[0]
    points = matrix.shape[1]
    operands = [order, coefficients, matrix, near]
    specs = [in_vmem()] * 4
    aliases = {}
    if result is not None:
        operands.append(result)
        specs.append(in_hbm())
        aliases = {4: 0}
    return pl.pallas_call(
        functools.partial(expand_kernel, flip),
        out_shape=jax.ShapeDtypeStruct((rows, points), jnp.bfloat16),
        in_specs=specs,
        out_specs=in_hbm(),
        input_output_aliases=aliases,
        scratch_shapes=[
            pltpu.VMEM((rows // 2, points), jnp.bfloat16),
            pltpu.SemaphoreType.DMA((1,)),
        ],
        cost_estimate=pl.CostEstimate(
            flops=4 * coefficients.size * points, bytes_accessed=0, transcendentals=0
        ),
        compiler_params=pltpu.CompilerParams(vmem_limit_bytes=16 << 20),
        name="expand1" if flip else "expand0",
    )(*operands)


def shards(
    densities, compress, level_a, level_b, expand, near_tiles, tile_pairs, tile_count, cluster_order
):
    rows, points = densities.shape
    rank = compress.shape[2]
    sections = level_a.shape[0]
    clusters = cluster_order.shape[1]
    width = points // clusters
    slots = near_tiles.shape[0]
    core = lax.axis_index("tgt").astype(jnp.int32)
    tiles = near_tiles.reshape(slots, 2 * width, width)
    ids = jnp.arange(clusters, dtype=jnp.int32)
    found = cluster_order[0][None, :] == tile_pairs[:, 0][:, None]
    places = jnp.sum(jnp.where(found, ids[None, :], 0), axis=1)
    table = jnp.stack([places, tile_pairs[:, 1]])
    count = jnp.minimum(tile_count, slots)
    cut = slots * 3 // 5
    half_rows = rows // 2

    product = jnp.dot(
        densities, compress.reshape(points, 2 * rank), preferred_element_type=jnp.float32
    )
    upper, lower = product[:half_rows], product[half_rows:]
    quarter = half_rows // 2
    first_core = core == 0
    keep, send = [], []
    for value in (upper[:, :rank] - lower[:, rank:], upper[:, rank:] + lower[:, :rank]):
        keep.append(jnp.where(first_core, value[:quarter], value[quarter:]))
        send.append(jnp.where(first_core, value[quarter:], value[:quarter]))
    keep = jnp.concatenate(keep, axis=0)
    arrived = swapped(jnp.concatenate(send, axis=0).astype(jnp.bfloat16), "tgt", 0)
    coefficients = (keep + arrived.astype(jnp.float32)).astype(jnp.bfloat16)

    def both(matrix):
        planes = matrix.transpose(0, 2, 1, 3)
        other = swapped(planes, "tgt", 0)
        joined = jnp.concatenate([planes, other], axis=3)
        return joined.reshape(sections, 2 * rank, rank)

    own_matrices, partner_matrices = both(level_a), both(level_b)
    for section in range(sections):
        partner = swapped(coefficients, "src", section)
        if section == 0:
            mixed, near = first_call(densities, clusters)
        elif section == 1:
            near = tiles_call(0, cut, table, count, mixed, tiles, near)
        elif section == 2:
            near = tiles_call(cut, slots, table, count, mixed, tiles, near)
        own = jnp.dot(
            paired(coefficients), own_matrices[section], preferred_element_type=jnp.float32
        )
        own = lax.optimization_barrier(own)
        updated = own + jnp.dot(
            paired(partner), partner_matrices[section], preferred_element_type=jnp.float32
        )
        updated = updated.astype(jnp.bfloat16)
        turned = jnp.concatenate([updated[:, rank // 2 :], updated[:, : rank // 2]], axis=1)
        coefficients = jnp.where(first_core, updated, turned)
    others = swapped(coefficients, "tgt", 0)
    matrix = expand.transpose(1, 0, 2).reshape(2 * rank, points)
    result = expand_call(False, cluster_order, coefficients, matrix, near, None)
    return expand_call(True, cluster_order, others, matrix, near, result)


def solution(mesh):
    placed = (
        P("grp", ("src", "tgt")),
        P(("grp", "src", "tgt"), None, None),
        P("grp", "src", None, "tgt"),
        P("grp", "src", None, "tgt"),
        P(("grp", "src"), None, "tgt"),
        P(("grp", "src", "tgt"), None, None, None),
        P(("grp", "src", "tgt"), None),
        P(("grp", "src", "tgt")),
        P(("grp", "src", "tgt"), None),
    )
    return jax.shard_map(
        shards, mesh=mesh, in_specs=placed, out_specs=P("grp", ("src", "tgt")), check_vma=False
    )
```

profile of v0, /device:TPU:3, one launch (start us, length us, event | category | flops | bytes accessed | tf_op | source)
XLA Modules:
  0.0 31.6 jit_solution(27892072181631401)
XLA Ops:
  0.0 2.1 %copy.20 = bf16[256,8,2,256]{3,1,2,0:T(8,128)(2,1)S(1)} copy(bf16[256,8,2,256]{3,2,1,0:T(2,128)(2,1)} %bitcast.36) | data formatting | bytes 4194304
  2.1 0.7 %fusion.62 = f32[256,512]{1,0:T(8,128)S(1)} fusion(bf16[256,2048]{1,0:T(8,128)(2,1)S(1)} %copy-done.1, bf16[2048,512]{1,0:T(8,128)(2,1)S(1)} %bitcast.38), kind=kOutput, calls=%fused_computation.98 | convolution fusion | flops 536870912 | bytes 3670016 | tf_op jit(solution)/shard_map/dot_general | solution.py:196
  2.8 0.0 copy-start.4
  2.9 0.0 copy-start.2
  3.0 0.7 %collective-permute-start = (bf16[128,256]{1,0:T(8,128)(2,1)S(1)}, bf16[128,256]{1,0:T(8,128)(2,1)S(1)}, u32[]{:S(2)}, u32[]{:S(2)}) collective-permute-start(bf16[128,256]{1,0:T(8,128)(2,1)S(1)} %pad_maximum_fusion.2), channel_id=1, source_target_pairs={{0,1},{1,0},{2,3},{3,2},{4,5},{5,4},{6,7},{7,6},{8,9},{9,8},{10,11... | collective-permute-start | bytes 196616 | tf_op jit(solution)/shard_map/ppermute | solution.py:30
  3.7 1.0 %copy.24 = bf16[3,256,2,128]{3,1,2,0:T(8,128)(2,1)S(1)} copy(bf16[3,256,2,128]{3,2,1,0:T(2,128)(2,1)} %param.11) | data formatting | bytes 786432 | tf_op args[2]
  4.8 0.2 collective-permute-start.1
  5.0 1.0 %copy.23 = bf16[3,256,2,128]{3,1,2,0:T(8,128)(2,1)S(1)} copy(bf16[3,256,2,128]{3,2,1,0:T(2,128)(2,1)} %param.12) | data formatting | bytes 786432 | tf_op args[3]
  6.0 0.4 %collective-permute-start.3 = (bf16[3,2,256,128]{3,2,1,0:T(8,128)(2,1)S(1)}, bf16[3,2,256,128]{3,2,1,0:T(8,128)(2,1)S(1)}, u32[]{:S(2)}, u32[]{:S(2)}) collective-permute-start(bf16[3,2,256,128]{3,2,1,0:T(8,128)(2,1)S(1)} %bitcast.39), channel_id=1, source_target_pairs={{0,1},{1,0},{2,3},{3,2},{4,5},{5,4},{6,7},{7,6},{8,9},{9,8},{10,11... | collective-permute-start | bytes 1179656 | tf_op jit(solution)/shard_map/ppermute | solution.py:30
  6.5 0.1 select_reduce_fusion
  6.6 0.8 %weave.1 = (bf16[16,256,256]{2,1,0:T(8,128)(2,1)S(1)}, f32[256,2176]{1,0:T(8,128)S(1)}) custom-call(bf16[256,2048]{1,0:T(8,128)(2,1)S(1)} %copy-done.1), custom_call_target="tpu_custom_call" | custom-call | flops 268435456 | tf_op jit(solution)/shard_map/weave/pallas_call | solution.py:75
  8.1 0.9 %copy.19 = bf16[2,256,2048]{2,1,0:T(8,128)(2,1)S(1)} copy(bf16[2,256,2048]{2,0,1:T(2,128)(2,1)S(1)} %bitcast.37) | data formatting | bytes 4194304 | tf_op jit(solution)/shard_map/transpose | solution.py:236
  9.0 1.3 %copy-done = bf16[64,128,2,128]{3,2,1,0:T(2,128)(2,1)S(1)} copy-done((bf16[64,128,2,128]{3,2,1,0:T(2,128)(2,1)S(1)}, bf16[64,128,2,128]{3,2,1,0:T(2,128)(2,1)}, u32[]{:S(2)}) %copy-start) | copy-done | bytes 4194328
  10.3 2.1 %tiles.2.before = f32[256,2176]{1,0:T(8,128)S(1)} custom-call(s32[2,64]{1,0:T(2,128)S(1)} %pad_add_fusion.table_ref, s32[1]{0:T(128)S(6)} %min.3.count_ref, bf16[16,256,256]{2,1,0:T(8,128)(2,1)S(1)} %get-tuple-element.7.mixed_ref, bf16[64,256,128]{2,1,0:T(8,128)(2,1)S(1)} %bitcast.33, ...), custom_call_target="tpu_custom_call", output_to_operand_aliasing={{}: (4, {})} | custom-call | flops 637534208 | tf_op jit(solution)/shard_map/tiles/pallas_call | solution.py:94
  12.4 0.9 %collective-permute-start.2 = (bf16[128,256]{1,0:T(8,128)(2,1)S(1)}, bf16[128,256]{1,0:T(8,128)(2,1)S(1)}, u32[]{:S(2)}, u32[]{:S(2)}) collective-permute-start(bf16[128,256]{1,0:T(8,128)(2,1)S(1)} %fusion.6), channel_id=1, source_target_pairs={{0,2},{2,0},{4,6},{6,4},{8,10},{10,8},{12,14},{14,12},{1,3},{3,1},... | collective-permute-start | bytes 196616 | tf_op jit(solution)/shard_map/ppermute | solution.py:30
  13.3 3.2 %collective-permute-done.2 = bf16[128,256]{1,0:T(8,128)(2,1)S(1)} collective-permute-done((bf16[128,256]{1,0:T(8,128)(2,1)S(1)}, bf16[128,256]{1,0:T(8,128)(2,1)S(1)}, u32[]{:S(2)}, u32[]{:S(2)}) %collective-permute-start.2) | collective-permute-done | bytes 65568 | tf_op jit(solution)/shard_map/ppermute | solution.py:30
  16.5 0.1 fusion.5
  16.6 0.2 fusion.7
  16.8 0.1 pad_maximum_fusion
  16.9 0.2 fusion
  17.2 0.9 %collective-permute-start.4 = (bf16[128,256]{1,0:T(8,128)(2,1)S(1)}, bf16[128,256]{1,0:T(8,128)(2,1)S(1)}, u32[]{:S(2)}, u32[]{:S(2)}) collective-permute-start(bf16[128,256]{1,0:T(8,128)(2,1)S(1)} %maximum_select_fusion), channel_id=1, source_target_pairs={{0,4},{2,6},{4,0},{6,2},{8,12},{10,14},{12,8},{14,10},{1,5},{3,7},... | collective-permute-start | bytes 196616 | tf_op jit(solution)/shard_map/ppermute | solution.py:30
  18.1 0.2 fusion.22
  18.3 2.1 %collective-permute-done.4 = bf16[128,256]{1,0:T(8,128)(2,1)S(1)} collective-permute-done((bf16[128,256]{1,0:T(8,128)(2,1)S(1)}, bf16[128,256]{1,0:T(8,128)(2,1)S(1)}, u32[]{:S(2)}, u32[]{:S(2)}) %collective-permute-start.4) | collective-permute-done | bytes 65568 | tf_op jit(solution)/shard_map/ppermute | solution.py:30
  20.4 0.2 fusion.1
  20.6 1.4 %collective-permute-start.5 = (bf16[128,256]{1,0:T(8,128)(2,1)S(1)}, bf16[128,256]{1,0:T(8,128)(2,1)S(1)}, u32[]{:S(2)}, u32[]{:S(2)}) collective-permute-start(bf16[128,256]{1,0:T(8,128)(2,1)S(1)} %maximum_select_fusion.1), channel_id=1, source_target_pairs={{0,8},{2,10},{4,12},{6,14},{8,0},{10,2},{12,4},{14,6},{1,9},{3,11}... | collective-permute-start | bytes 196616 | tf_op jit(solution)/shard_map/ppermute | solution.py:30
  22.0 0.2 fusion.37
  22.2 3.2 %collective-permute-done.5 = bf16[128,256]{1,0:T(8,128)(2,1)S(1)} collective-permute-done((bf16[128,256]{1,0:T(8,128)(2,1)S(1)}, bf16[128,256]{1,0:T(8,128)(2,1)S(1)}, u32[]{:S(2)}, u32[]{:S(2)}) %collective-permute-start.5) | collective-permute-done | bytes 65568 | tf_op jit(solution)/shard_map/ppermute | solution.py:30
  25.4 0.2 fusion.45
  25.7 2.2 %collective-permute-start.6 = (bf16[128,256]{1,0:T(8,128)(2,1)S(1)}, bf16[128,256]{1,0:T(8,128)(2,1)S(1)}, u32[]{:S(2)}, u32[]{:S(2)}) collective-permute-start(bf16[128,256]{1,0:T(8,128)(2,1)S(1)} %maximum_select_fusion.2.coeff_ref), channel_id=1, source_target_pairs={{0,1},{1,0},{2,3},{3,2},{4,5},{5,4},{6,7},{7,6},{8,9},{9,8},{10,11... | collective-permute-start | bytes 196616 | tf_op jit(solution)/shard_map/ppermute | solution.py:30
  27.9 1.5 %tiles.3.near_ref = f32[256,2176]{1,0:T(8,128)S(1)} custom-call(s32[2,64]{1,0:T(2,128)S(1)} %pad_add_fusion.table_ref, s32[1]{0:T(128)S(6)} %min.3.count_ref, bf16[16,256,256]{2,1,0:T(8,128)(2,1)S(1)} %get-tuple-element.7.mixed_ref, bf16[64,256,128]{2,1,0:T(8,128)(2,1)S(1)} %bitcast.34, f32[256,2176]{1,0:T(8,128)S(1)} %tiles.2.before), custom_call_target="tpu_custom_call", output_to_operand_aliasing={{}: (4, {})} | custom-call | flops 436207616 | tf_op jit(solution)/shard_map/tiles/pallas_call | solution.py:94
  29.3 1.1 %expand0.1.refs_0_ = bf16[256,2048]{1,0:T(8,128)(2,1)} custom-call(s32[1,16]{1,0:T(1,128)S(1)} %copy-done.2, bf16[128,256]{1,0:T(8,128)(2,1)S(1)} %maximum_select_fusion.2.coeff_ref, bf16[512,2048]{1,0:T(8,128)(2,1)S(1)} %bitcast.31, f32[256,2176]{1,0:T(8,128)S(1)} %tiles.3.near_ref), custom_call_target="tpu_custom_call" | custom-call | flops 268435456 | tf_op jit(solution)/shard_map/expand0/pallas_call | solution.py:159
  30.5 1.2 %expand1.1 = bf16[256,2048]{1,0:T(8,128)(2,1)} custom-call(s32[1,16]{1,0:T(1,128)S(1)} %copy-done.2, bf16[128,256]{1,0:T(8,128)(2,1)S(1)} %collective-permute-done.6.coeff_ref, bf16[512,2048]{1,0:T(8,128)(2,1)S(1)} %bitcast.32, f32[256,2176]{1,0:T(8,128)S(1)} %tiles.3.near_ref, bf16[256,2048]{1,0:T(8,128)(2,1)} %expand0.1.refs_0_), custom_call_target="tpu_custom_call", output_to_operand_aliasing={{}: (4, {})} | custom-call | flops 268435456 | tf_op jit(solution)/shard_map/expand1/pallas_call | solution.py:159
  (31 shorter events, 0.3 us)
Async XLA Ops:
  0.0 2.1 %copy-start.1 = (bf16[256,2048]{1,0:T(8,128)(2,1)S(1)}, bf16[256,2048]{1,0:T(8,128)(2,1)}, u32[]{:S(2)}) copy-start(bf16[256,2048]{1,0:T(8,128)(2,1)} %dens_ref.1) | copy-start | bytes 3145732
  2.8 3.6 %copy-start.4 = (s32[64,2]{0,1:T(2,128)S(1)}, s32[64,2]{0,1:T(2,128)}, u32[]{:S(2)}) copy-start(s32[64,2]{0,1:T(2,128)} %param.15) | copy-start | bytes 1540
  2.9 3.6 %copy-start.2 = (s32[1,16]{1,0:T(1,128)S(1)}, s32[1,16]{1,0:T(1,128)}, u32[]{:S(2)}) copy-start(s32[1,16]{1,0:T(1,128)} %order_ref.3) | copy-start | bytes 196
  2.9 5.2 %copy-start.3 = (bf16[256,2,2048]{2,1,0:T(2,128)(2,1)S(1)}, bf16[256,2,2048]{2,1,0:T(2,128)(2,1)}, u32[]{:S(2)}) copy-start(bf16[256,2,2048]{2,1,0:T(2,128)(2,1)} %param.13) | copy-start | bytes 6291460
  3.0 9.4 %collective-permute-start = (bf16[128,256]{1,0:T(8,128)(2,1)S(1)}, bf16[128,256]{1,0:T(8,128)(2,1)S(1)}, u32[]{:S(2)}, u32[]{:S(2)}) collective-permute-start(bf16[128,256]{1,0:T(8,128)(2,1)S(1)} %pad_maximum_fusion.2), channel_id=1, source_target_pairs={{0,1},{1,0},{2,3},{3,2},{4,5},{5,4},{6,7},{7,6},{8,9},{9,8},{10,11... | collective-permute-start | bytes 196616 | tf_op jit(solution)/shard_map/ppermute | solution.py:30
  4.8 11.8 %collective-permute-start.1 = (bf16[3,2,256,128]{3,2,1,0:T(8,128)(2,1)S(1)}, bf16[3,2,256,128]{3,2,1,0:T(8,128)(2,1)S(1)}, u32[]{:S(2)}, u32[]{:S(2)}) collective-permute-start(bf16[3,2,256,128]{3,2,1,0:T(8,128)(2,1)S(1)} %bitcast.41), channel_id=1, source_target_pairs={{0,1},{1,0},{2,3},{3,2},{4,5},{5,4},{6,7},{7,6},{8,9},{9,8},{10,11... | collective-permute-start | bytes 1179656 | tf_op jit(solution)/shard_map/ppermute | solution.py:30
  6.0 10.8 %collective-permute-start.3 = (bf16[3,2,256,128]{3,2,1,0:T(8,128)(2,1)S(1)}, bf16[3,2,256,128]{3,2,1,0:T(8,128)(2,1)S(1)}, u32[]{:S(2)}, u32[]{:S(2)}) collective-permute-start(bf16[3,2,256,128]{3,2,1,0:T(8,128)(2,1)S(1)} %bitcast.39), channel_id=1, source_target_pairs={{0,1},{1,0},{2,3},{3,2},{4,5},{5,4},{6,7},{7,6},{8,9},{9,8},{10,11... | collective-permute-start | bytes 1179656 | tf_op jit(solution)/shard_map/ppermute | solution.py:30
  8.1 2.2 %copy-start = (bf16[64,128,2,128]{3,2,1,0:T(2,128)(2,1)S(1)}, bf16[64,128,2,128]{3,2,1,0:T(2,128)(2,1)}, u32[]{:S(2)}) copy-start(bf16[64,128,2,128]{3,2,1,0:T(2,128)(2,1)} %param.14) | copy-start | bytes 12582916
  12.4 4.1 %collective-permute-start.2 = (bf16[128,256]{1,0:T(8,128)(2,1)S(1)}, bf16[128,256]{1,0:T(8,128)(2,1)S(1)}, u32[]{:S(2)}, u32[]{:S(2)}) collective-permute-start(bf16[128,256]{1,0:T(8,128)(2,1)S(1)} %fusion.6), channel_id=1, source_target_pairs={{0,2},{2,0},{4,6},{6,4},{8,10},{10,8},{12,14},{14,12},{1,3},{3,1},... | collective-permute-start | bytes 196616 | tf_op jit(solution)/shard_map/ppermute | solution.py:30
  17.2 3.2 %collective-permute-start.4 = (bf16[128,256]{1,0:T(8,128)(2,1)S(1)}, bf16[128,256]{1,0:T(8,128)(2,1)S(1)}, u32[]{:S(2)}, u32[]{:S(2)}) collective-permute-start(bf16[128,256]{1,0:T(8,128)(2,1)S(1)} %maximum_select_fusion), channel_id=1, source_target_pairs={{0,4},{2,6},{4,0},{6,2},{8,12},{10,14},{12,8},{14,10},{1,5},{3,7},... | collective-permute-start | bytes 196616 | tf_op jit(solution)/shard_map/ppermute | solution.py:30
  20.6 4.8 %collective-permute-start.5 = (bf16[128,256]{1,0:T(8,128)(2,1)S(1)}, bf16[128,256]{1,0:T(8,128)(2,1)S(1)}, u32[]{:S(2)}, u32[]{:S(2)}) collective-permute-start(bf16[128,256]{1,0:T(8,128)(2,1)S(1)} %maximum_select_fusion.1), channel_id=1, source_target_pairs={{0,8},{2,10},{4,12},{6,14},{8,0},{10,2},{12,4},{14,6},{1,9},{3,11}... | collective-permute-start | bytes 196616 | tf_op jit(solution)/shard_map/ppermute | solution.py:30
  25.7 4.8 %collective-permute-start.6 = (bf16[128,256]{1,0:T(8,128)(2,1)S(1)}, bf16[128,256]{1,0:T(8,128)(2,1)S(1)}, u32[]{:S(2)}, u32[]{:S(2)}) collective-permute-start(bf16[128,256]{1,0:T(8,128)(2,1)S(1)} %maximum_select_fusion.2.coeff_ref), channel_id=1, source_target_pairs={{0,1},{1,0},{2,3},{3,2},{4,5},{5,4},{6,7},{7,6},{8,9},{9,8},{10,11... | collective-permute-start | bytes 196616 | tf_op jit(solution)/shard_map/ppermute | solution.py:30
where the time goes:
time: 31.8 us; the launch traced here: 31.6 us
  waiting for transfers between devices  8.55 us (27%)
  Pallas kernels  6.68 us (21%)
  starting transfers between devices  6.64 us (21%)
  local copies, waits for them, and re-layouts  6.44 us (20%)
  matrix products  1.83 us (6%)
  between operations  0.99 us (3%)
  other arithmetic  0.51 us (2%)
    ppermute x7, waiting for transfers between devices, swapped(): return lax.ppermute(value, axis, pairs)  8.55 us
    ppermute x7, starting transfers between devices, swapped(): return lax.ppermute(value, axis, pairs)  6.64 us
    unnamed x13, local copies, waits for them, and re-layouts  5.52 us
    pallas_call x2, Pallas kernels, tiles_call(): pl.pallas_call(functools.partial(tiles_kernel, first, last), out_shape=ja...  3.56 us
    pallas_call x2, Pallas kernels, expand_call(): pl.pallas_call(functools.partial(expand_kernel, flip), out_shape=jax.Shap...  2.3 us
    transpose x1, local copies, waits for them, and re-layouts, shards(): matrix = expand.transpose(1, 0, 2).reshape(2 * rank, points)  0.89 us
    pallas_call x1, Pallas kernels, first_call(): pl.pallas_call(first_kernel, out_shape=(jax.ShapeDtypeStruct((clusters, r...  0.82 us
    dot_general x1, matrix products, shards(): jnp.dot(densities, compress.reshape(points, 2 * rank), preferred_element_...  0.7 us
  transfers between devices with their start and end apart: 7, of which 3 were waited for; matrix products, arithmetic and copies ran while one was open for 12% of the time, Pallas kernels for 17%

commit v1 on v0

--- a/solution.py
+++ b/solution.py
@@ -9,7 +9,7 @@
 
 
 EXPAND_CHUNKS = 4
-UNROLL = 16
+UNROLL = 64
 
 
 def in_vmem():
@@ -36,6 +36,41 @@
     return jnp.concatenate(
         [jnp.concatenate([upper, -lower], axis=1), jnp.concatenate([lower, upper], axis=1)], axis=0
     )
+
+
+def partial_kernel(dens_ref, flat_ref, keep_ref, send_ref, total):
+    half, rank = keep_ref.shape
+    quarter = half // 2
+    core = lax.axis_index("tgt")
+    product = jnp.dot(dens_ref[...], flat_ref[...], preferred_element_type=jnp.float32)
+    total[:half, :] = product[:half, :rank] - product[half:, rank:]
+    total[half:, :] = product[:half, rank:] + product[half:, :rank]
+    for part in range(2):
+        inner = slice(part * quarter, (part + 1) * quarter)
+        mine = pl.ds(pl.multiple_of((2 * part + core) * quarter, quarter), quarter)
+        other = pl.ds(pl.multiple_of((2 * part + 1 - core) * quarter, quarter), quarter)
+        keep_ref[inner, :] = total[mine, :]
+        send_ref[inner, :] = total[other, :].astype(send_ref.dtype)
+
+
+def partial_call(densities, flat):
+    rows, points = densities.shape
+    rank = flat.shape[1] // 2
+    return pl.pallas_call(
+        partial_kernel,
+        out_shape=(
+            jax.ShapeDtypeStruct((rows // 2, rank), jnp.float32),
+            jax.ShapeDtypeStruct((rows // 2, rank), jnp.bfloat16),
+        ),
+        in_specs=[in_vmem(), in_vmem()],
+        out_specs=(in_vmem(), in_vmem()),
+        scratch_shapes=[pltpu.VMEM((rows, rank), jnp.float32)],
+        cost_estimate=pl.CostEstimate(
+            flops=4 * rows * points * rank, bytes_accessed=0, transcendentals=0
+        ),
+        compiler_params=pltpu.CompilerParams(vmem_limit_bytes=16 << 20),
+        name="partial",
+    )(densities, flat)
 
 
 def first_kernel(dens_ref, mixed_ref, total, weave):
@@ -177,7 +212,7 @@
 def shards(
     densities, compress, level_a, level_b, expand, near_tiles, tile_pairs, tile_count, cluster_order
 ):
-    rows, points = densities.shape
+    _, points = densities.shape
     rank = compress.shape[2]
     sections = level_a.shape[0]
     clusters = cluster_order.shape[1]
@@ -190,30 +225,27 @@
     places = jnp.sum(jnp.where(found, ids[None, :], 0), axis=1)
     table = jnp.stack([places, tile_pairs[:, 1]])
     count = jnp.minimum(tile_count, slots)
-    cut = slots * 3 // 5
-    half_rows = rows // 2
-
-    product = jnp.dot(
-        densities, compress.reshape(points, 2 * rank), preferred_element_type=jnp.float32
-    )
-    upper, lower = product[:half_rows], product[half_rows:]
-    quarter = half_rows // 2
+    cut = slots * 3 // 4
+
     first_core = core == 0
-    keep, send = [], []
-    for value in (upper[:, :rank] - lower[:, rank:], upper[:, rank:] + lower[:, :rank]):
-        keep.append(jnp.where(first_core, value[:quarter], value[quarter:]))
-        send.append(jnp.where(first_core, value[quarter:], value[:quarter]))
-    keep = jnp.concatenate(keep, axis=0)
-    arrived = swapped(jnp.concatenate(send, axis=0).astype(jnp.bfloat16), "tgt", 0)
+    keep, send = partial_call(densities, compress.reshape(points, 2 * rank))
+    arrived = swapped(send, "tgt", 0)
     coefficients = (keep + arrived.astype(jnp.float32)).astype(jnp.bfloat16)
 
-    def both(matrix):
+    def both(matrix, earlier):
         planes = matrix.transpose(0, 2, 1, 3)
         other = swapped(planes, "tgt", 0)
-        joined = jnp.concatenate([planes, other], axis=3)
-        return joined.reshape(sections, 2 * rank, rank)
-
-    own_matrices, partner_matrices = both(level_a), both(level_b)
+        if earlier is not None:
+            other, earlier = lax.optimization_barrier((other, earlier))
+        joined = jnp.where(
+            first_core,
+            jnp.concatenate([planes, other], axis=3),
+            jnp.concatenate([other, planes], axis=3),
+        )
+        return joined.reshape(sections, 2 * rank, rank), earlier
+
+    own_matrices, _ = both(level_a, None)
+    partner_matrices, own_matrices = both(level_b, own_matrices)
     for section in range(sections):
         partner = swapped(coefficients, "src", section)
         if section == 0:
@@ -229,9 +261,7 @@
         updated = own + jnp.dot(
             paired(partner), partner_matrices[section], preferred_element_type=jnp.float32
         )
-        updated = updated.astype(jnp.bfloat16)
-        turned = jnp.concatenate([updated[:, rank // 2 :], updated[:, : rank // 2]], axis=1)
-        coefficients = jnp.where(first_core, updated, turned)
+        coefficients = updated.astype(jnp.bfloat16)
     others = swapped(coefficients, "tgt", 0)
     matrix = expand.transpose(1, 0, 2).reshape(2 * rank, points)
     result = expand_call(False, cluster_order, coefficients, matrix, near, None)

time: 31.8 us -> 30.5 us (0.959)
  the two profiles are of different devices: /device:TPU:3 before, /device:TPU:29 now
where the time goes in v1:
time: 30.5 us; the launch traced here: 30.3 us
  waiting for transfers between devices  10.5 us (34%)
  Pallas kernels  6.65 us (22%)
  starting transfers between devices  5.28 us (17%)
  local copies, waits for them, and re-layouts  5.18 us (17%)
  matrix products  1.14 us (4%)
  between operations  0.89 us (3%)
  other arithmetic  0.7 us (2%)
    ppermute x7, waiting for transfers between devices, swapped(): return lax.ppermute(value, axis, pairs)  10.5 us
    ppermute x7, starting transfers between devices, swapped(): return lax.ppermute(value, axis, pairs)  5.28 us
    unnamed x13, local copies, waits for them, and re-layouts  4.25 us
    pallas_call x2, Pallas kernels, tiles_call(): pl.pallas_call(functools.partial(tiles_kernel, first, last), out_shape=ja...  2.86 us
    pallas_call x2, Pallas kernels, expand_call(): pl.pallas_call(functools.partial(expand_kernel, flip), out_shape=jax.Shap...  2.24 us
    transpose x1, local copies, waits for them, and re-layouts, shards(): matrix = expand.transpose(1, 0, 2).reshape(2 * rank, points)  0.88 us
    pallas_call x1, Pallas kernels, first_call(): pl.pallas_call(first_kernel, out_shape=(jax.ShapeDtypeStruct((clusters, r...  0.81 us
    pallas_call x1, Pallas kernels, partial_call(): pl.pallas_call(partial_kernel, out_shape=(jax.ShapeDtypeStruct((rows // 2...  0.74 us
  transfers between devices with their start and end apart: 7, of which 3 were waited for; matrix products, arithmetic and copies ran while one was open for 16% of the time, Pallas kernels for 18%

profile of v1, /device:TPU:29, one launch (start us, length us, event | category | flops | bytes accessed | tf_op | source)
XLA Modules:
  0.0 30.3 jit_solution(15148671348166255973)
XLA Ops:
  0.0 1.0 %copy.25 = bf16[3,256,2,128]{3,1,2,0:T(8,128)(2,1)S(1)} copy(bf16[3,256,2,128]{3,2,1,0:T(2,128)(2,1)} %param.11) | data formatting | bytes 786432 | tf_op args[2]
  1.1 0.7 %collective-permute-start.2 = (bf16[3,2,256,128]{3,2,1,0:T(8,128)(2,1)S(1)}, bf16[3,2,256,128]{3,2,1,0:T(8,128)(2,1)S(1)}, u32[]{:S(2)}, u32[]{:S(2)}) collective-permute-start(bf16[3,2,256,128]{3,2,1,0:T(8,128)(2,1)S(1)} %bitcast.44), channel_id=1, source_target_pairs={{0,1},{1,0},{2,3},{3,2},{4,5},{5,4},{6,7},{7,6},{8,9},{9,8},{10,11... | collective-permute-start | bytes 1179656 | tf_op jit(solution)/shard_map/ppermute | solution.py:30
  1.8 1.0 %copy.24 = bf16[3,256,2,128]{3,1,2,0:T(8,128)(2,1)S(1)} copy(bf16[3,256,2,128]{3,2,1,0:T(2,128)(2,1)} %param.12) | data formatting | bytes 786432 | tf_op args[3]
  2.8 0.1 collective-permute-start.1
  2.9 2.1 %copy.20 = bf16[256,8,2,256]{3,1,2,0:T(8,128)(2,1)S(1)} copy(bf16[256,8,2,256]{3,2,1,0:T(2,128)(2,1)} %bitcast.40) | data formatting | bytes 4194304
  5.1 0.0 copy-start.4
  5.1 0.0 copy-start.2
  5.1 0.7 %partial.1 = (f32[128,256]{1,0:T(8,128)S(1)}, bf16[128,256]{1,0:T(8,128)(2,1)S(1)}) custom-call(bf16[256,2048]{1,0:T(8,128)(2,1)S(1)} %copy-done.1, bf16[2048,512]{1,0:T(8,128)(2,1)S(1)} %bitcast.38), custom_call_target="tpu_custom_call" | custom-call | flops 536870912 | tf_op jit(solution)/shard_map/partial/pallas_call | solution.py:59
  5.8 0.6 %collective-permute-start = (bf16[128,256]{1,0:T(8,128)(2,1)S(1)}, bf16[128,256]{1,0:T(8,128)(2,1)S(1)}, u32[]{:S(2)}, u32[]{:S(2)}) collective-permute-start(bf16[128,256]{1,0:T(8,128)(2,1)S(1)} %get-tuple-element.12), channel_id=1, source_target_pairs={{0,1},{1,0},{2,3},{3,2},{4,5},{5,4},{6,7},{7,6},{8,9},{9,8},{10,11... | collective-permute-start | bytes 196616 | tf_op jit(solution)/shard_map/ppermute | solution.py:30
  6.4 0.1 select_reduce_fusion
  7.2 0.8 %weave.1 = (bf16[16,256,256]{2,1,0:T(8,128)(2,1)S(1)}, f32[256,2176]{1,0:T(8,128)S(1)}) custom-call(bf16[256,2048]{1,0:T(8,128)(2,1)S(1)} %copy-done.1), custom_call_target="tpu_custom_call" | custom-call | flops 268435456 | tf_op jit(solution)/shard_map/weave/pallas_call | solution.py:110
  8.0 0.3 collective-permute-start.3
  8.3 3.4 %collective-permute-done.3 = bf16[128,256]{1,0:T(8,128)(2,1)S(1)} collective-permute-done((bf16[128,256]{1,0:T(8,128)(2,1)S(1)}, bf16[128,256]{1,0:T(8,128)(2,1)S(1)}, u32[]{:S(2)}, u32[]{:S(2)}) %collective-permute-start.3) | collective-permute-done | bytes 65568 | tf_op jit(solution)/shard_map/ppermute | solution.py:30
  11.7 0.3 maximum_select_fusion
  12.0 0.2 fusion.7
  12.2 0.3 maximum_select_fusion.1
  12.5 0.1 fusion.60
  12.5 0.2 fusion
  12.8 0.2 collective-permute-start.4
  13.0 0.2 fusion.5
  13.2 2.7 %collective-permute-done.4 = bf16[128,256]{1,0:T(8,128)(2,1)S(1)} collective-permute-done((bf16[128,256]{1,0:T(8,128)(2,1)S(1)}, bf16[128,256]{1,0:T(8,128)(2,1)S(1)}, u32[]{:S(2)}, u32[]{:S(2)}) %collective-permute-start.4) | collective-permute-done | bytes 65568 | tf_op jit(solution)/shard_map/ppermute | solution.py:30
  16.0 0.2 fusion.1
  16.2 0.1 collective-permute-start.5
  16.3 0.2 fusion.3
  16.5 4.3 %collective-permute-done.5 = bf16[128,256]{1,0:T(8,128)(2,1)S(1)} collective-permute-done((bf16[128,256]{1,0:T(8,128)(2,1)S(1)}, bf16[128,256]{1,0:T(8,128)(2,1)S(1)}, u32[]{:S(2)}, u32[]{:S(2)}) %collective-permute-start.5) | collective-permute-done | bytes 65568 | tf_op jit(solution)/shard_map/ppermute | solution.py:30
  20.9 0.2 fusion.2.coeff_ref
  21.0 3.3 %collective-permute-start.6 = (bf16[128,256]{1,0:T(8,128)(2,1)S(1)}, bf16[128,256]{1,0:T(8,128)(2,1)S(1)}, u32[]{:S(2)}, u32[]{:S(2)}) collective-permute-start(bf16[128,256]{1,0:T(8,128)(2,1)S(1)} %fusion.2.coeff_ref), channel_id=1, source_target_pairs={{0,1},{1,0},{2,3},{3,2},{4,5},{5,4},{6,7},{7,6},{8,9},{9,8},{10,11... | collective-permute-start | bytes 196616 | tf_op jit(solution)/shard_map/ppermute | solution.py:30
  24.3 2.0 %tiles.2.before = f32[256,2176]{1,0:T(8,128)S(1)} custom-call(s32[2,64]{1,0:T(2,128)S(1)} %pad_add_fusion.table_ref, s32[1]{0:T(128)S(6)} %min.3.count_ref, bf16[16,256,256]{2,1,0:T(8,128)(2,1)S(1)} %get-tuple-element.15.mixed_ref, bf16[64,256,128]{2,1,0:T(8,128)(2,1)S(1)} %bitcast.36, ...), custom_call_target="tpu_custom_call", output_to_operand_aliasing={{}: (4, {})} | custom-call | flops 805306368 | tf_op jit(solution)/shard_map/tiles/pallas_call | solution.py:129
  26.3 0.9 %copy.19 = bf16[2,256,2048]{2,1,0:T(8,128)(2,1)S(1)} copy(bf16[2,256,2048]{2,0,1:T(2,128)(2,1)S(1)} %bitcast.41) | data formatting | bytes 4194304 | tf_op jit(solution)/shard_map/transpose | solution.py:266
  27.2 0.8 %tiles.3.near_ref = f32[256,2176]{1,0:T(8,128)S(1)} custom-call(s32[2,64]{1,0:T(2,128)S(1)} %pad_add_fusion.table_ref, s32[1]{0:T(128)S(6)} %min.3.count_ref, bf16[16,256,256]{2,1,0:T(8,128)(2,1)S(1)} %get-tuple-element.15.mixed_ref, bf16[64,256,128]{2,1,0:T(8,128)(2,1)S(1)} %bitcast.37, f32[256,2176]{1,0:T(8,128)S(1)} %tiles.2.before), custom_call_target="tpu_custom_call", output_to_operand_aliasing={{}: (4, {})} | custom-call | flops 268435456 | tf_op jit(solution)/shard_map/tiles/pallas_call | solution.py:129
  28.1 1.1 %expand0.1.refs_0_ = bf16[256,2048]{1,0:T(8,128)(2,1)} custom-call(s32[1,16]{1,0:T(1,128)S(1)} %copy-done.2, bf16[128,256]{1,0:T(8,128)(2,1)S(1)} %fusion.2.coeff_ref, bf16[512,2048]{1,0:T(8,128)(2,1)S(1)} %bitcast.34, f32[256,2176]{1,0:T(8,128)S(1)} %tiles.3.near_ref), custom_call_target="tpu_custom_call" | custom-call | flops 268435456 | tf_op jit(solution)/shard_map/expand0/pallas_call | solution.py:194
  29.2 1.1 %expand1.1 = bf16[256,2048]{1,0:T(8,128)(2,1)} custom-call(s32[1,16]{1,0:T(1,128)S(1)} %copy-done.2, bf16[128,256]{1,0:T(8,128)(2,1)S(1)} %collective-permute-done.6.coeff_ref, bf16[512,2048]{1,0:T(8,128)(2,1)S(1)} %bitcast.35, f32[256,2176]{1,0:T(8,128)S(1)} %tiles.3.near_ref, bf16[256,2048]{1,0:T(8,128)(2,1)} %expand0.1.refs_0_), custom_call_target="tpu_custom_call", output_to_operand_aliasing={{}: (4, {})} | custom-call | flops 268435456 | tf_op jit(solution)/shard_map/expand1/pallas_call | solution.py:194
  (21 shorter events, 0.1 us)
Async XLA Ops:
  1.1 10.7 %collective-permute-start.2 = (bf16[3,2,256,128]{3,2,1,0:T(8,128)(2,1)S(1)}, bf16[3,2,256,128]{3,2,1,0:T(8,128)(2,1)S(1)}, u32[]{:S(2)}, u32[]{:S(2)}) collective-permute-start(bf16[3,2,256,128]{3,2,1,0:T(8,128)(2,1)S(1)} %bitcast.44), channel_id=1, source_target_pairs={{0,1},{1,0},{2,3},{3,2},{4,5},{5,4},{6,7},{7,6},{8,9},{9,8},{10,11... | collective-permute-start | bytes 1179656 | tf_op jit(solution)/shard_map/ppermute | solution.py:30
  2.8 9.1 %collective-permute-start.1 = (bf16[3,2,256,128]{3,2,1,0:T(8,128)(2,1)S(1)}, bf16[3,2,256,128]{3,2,1,0:T(8,128)(2,1)S(1)}, u32[]{:S(2)}, u32[]{:S(2)}) collective-permute-start(bf16[3,2,256,128]{3,2,1,0:T(8,128)(2,1)S(1)} %bitcast.42), channel_id=1, source_target_pairs={{0,1},{1,0},{2,3},{3,2},{4,5},{5,4},{6,7},{7,6},{8,9},{9,8},{10,11... | collective-permute-start | bytes 1179656 | tf_op jit(solution)/shard_map/ppermute | solution.py:30
  2.9 2.1 %copy-start.1 = (bf16[256,2048]{1,0:T(8,128)(2,1)S(1)}, bf16[256,2048]{1,0:T(8,128)(2,1)}, u32[]{:S(2)}) copy-start(bf16[256,2048]{1,0:T(8,128)(2,1)} %dens_ref.3) | copy-start | bytes 3145732
  5.1 1.3 %copy-start.4 = (s32[64,2]{0,1:T(2,128)S(1)}, s32[64,2]{0,1:T(2,128)}, u32[]{:S(2)}) copy-start(s32[64,2]{0,1:T(2,128)} %param.15) | copy-start | bytes 1540
  5.1 1.3 %copy-start.2 = (s32[1,16]{1,0:T(1,128)S(1)}, s32[1,16]{1,0:T(1,128)}, u32[]{:S(2)}) copy-start(s32[1,16]{1,0:T(1,128)} %order_ref.3) | copy-start | bytes 196
  5.8 2.1 %collective-permute-start = (bf16[128,256]{1,0:T(8,128)(2,1)S(1)}, bf16[128,256]{1,0:T(8,128)(2,1)S(1)}, u32[]{:S(2)}, u32[]{:S(2)}) collective-permute-start(bf16[128,256]{1,0:T(8,128)(2,1)S(1)} %get-tuple-element.12), channel_id=1, source_target_pairs={{0,1},{1,0},{2,3},{3,2},{4,5},{5,4},{6,7},{7,6},{8,9},{9,8},{10,11... | collective-permute-start | bytes 196616 | tf_op jit(solution)/shard_map/ppermute | solution.py:30
  8.0 3.7 %collective-permute-start.3 = (bf16[128,256]{1,0:T(8,128)(2,1)S(1)}, bf16[128,256]{1,0:T(8,128)(2,1)S(1)}, u32[]{:S(2)}, u32[]{:S(2)}) collective-permute-start(bf16[128,256]{1,0:T(8,128)(2,1)S(1)} %add_convert_fusion), channel_id=1, source_target_pairs={{0,2},{2,0},{4,6},{6,4},{8,10},{10,8},{12,14},{14,12},{1,3},{3,1},... | collective-permute-start | bytes 196616 | tf_op jit(solution)/shard_map/ppermute | solution.py:30
  12.5 11.8 %copy-start = (bf16[64,128,2,128]{3,2,1,0:T(2,128)(2,1)S(1)}, bf16[64,128,2,128]{3,2,1,0:T(2,128)(2,1)}, u32[]{:S(2)}) copy-start(bf16[64,128,2,128]{3,2,1,0:T(2,128)(2,1)} %param.14) | copy-start | bytes 12582916
  12.8 3.2 %collective-permute-start.4 = (bf16[128,256]{1,0:T(8,128)(2,1)S(1)}, bf16[128,256]{1,0:T(8,128)(2,1)S(1)}, u32[]{:S(2)}, u32[]{:S(2)}) collective-permute-start(bf16[128,256]{1,0:T(8,128)(2,1)S(1)} %fusion), channel_id=1, source_target_pairs={{0,4},{2,6},{4,0},{6,2},{8,12},{10,14},{12,8},{14,10},{1,5},{3,7},... | collective-permute-start | bytes 196616 | tf_op jit(solution)/shard_map/ppermute | solution.py:30
  16.2 4.7 %collective-permute-start.5 = (bf16[128,256]{1,0:T(8,128)(2,1)S(1)}, bf16[128,256]{1,0:T(8,128)(2,1)S(1)}, u32[]{:S(2)}, u32[]{:S(2)}) collective-permute-start(bf16[128,256]{1,0:T(8,128)(2,1)S(1)} %fusion.1), channel_id=1, source_target_pairs={{0,8},{2,10},{4,12},{6,14},{8,0},{10,2},{12,4},{14,6},{1,9},{3,11}... | collective-permute-start | bytes 196616 | tf_op jit(solution)/shard_map/ppermute | solution.py:30
  21.0 8.2 %collective-permute-start.6 = (bf16[128,256]{1,0:T(8,128)(2,1)S(1)}, bf16[128,256]{1,0:T(8,128)(2,1)S(1)}, u32[]{:S(2)}, u32[]{:S(2)}) collective-permute-start(bf16[128,256]{1,0:T(8,128)(2,1)S(1)} %fusion.2.coeff_ref), channel_id=1, source_target_pairs={{0,1},{1,0},{2,3},{3,2},{4,5},{5,4},{6,7},{7,6},{8,9},{9,8},{10,11... | collective-permute-start | bytes 196616 | tf_op jit(solution)/shard_map/ppermute | solution.py:30
  24.3 2.0 %copy-start.3 = (bf16[256,2,2048]{2,1,0:T(2,128)(2,1)S(1)}, bf16[256,2,2048]{2,1,0:T(2,128)(2,1)}, u32[]{:S(2)}) copy-start(bf16[256,2,2048]{2,1,0:T(2,128)(2,1)} %param.13) | copy-start | bytes 6291460

commit v2 on v1

--- a/solution.py
+++ b/solution.py
@@ -8,7 +8,7 @@
 from jax.sharding import PartitionSpec as P
 
 
-EXPAND_CHUNKS = 4
+EXPAND_CHUNKS = 8
 UNROLL = 64
 
 
@@ -87,7 +87,13 @@
     total[...] = jnp.zeros_like(total)
 
 
-def tiles_kernel(first, last, table_ref, count_ref, mixed_ref, tiles_ref, before, total):
+def tiles_kernel(first, last, table_ref, count_ref, mixed_ref, tiles_ref, before, *refs):
+    fetch = None
+    total = refs[0]
+    if len(refs) > 1:
+        expand_hbm, total, held_ref, sem = refs
+        fetch = pltpu.make_async_copy(expand_hbm, held_ref, sem.at[0])
+        fetch.start()
     clusters = mixed_ref.shape[0]
     width = tiles_ref.shape[2]
     count = count_ref[0]
@@ -102,6 +108,8 @@
                 total[:, columns] += jnp.dot(
                     mixed_ref[table[1, slot]], tiles_ref[slot], preferred_element_type=jnp.float32
                 )
+    if fetch is not None:
+        fetch.wait()
 
 
 def first_call(densities, clusters):
@@ -124,14 +132,24 @@
     )(densities)
 
 
-def tiles_call(first, last, table, count, mixed, tiles, total):
+def tiles_call(first, last, table, count, mixed, tiles, total, expand=None):
     depth, width = tiles.shape[1:]
+    operands = [table, count, mixed, tiles, total]
+    specs = [in_vmem(), in_smem(), in_vmem(), in_vmem(), in_vmem()]
+    shapes = [jax.ShapeDtypeStruct(total.shape, total.dtype)]
+    scratch = []
+    if expand is not None:
+        operands.append(pltpu.with_memory_space_constraint(expand, pltpu.HBM))
+        specs.append(in_hbm())
+        shapes.append(jax.ShapeDtypeStruct(expand.shape, expand.dtype))
+        scratch = [pltpu.SemaphoreType.DMA((1,))]
     return pl.pallas_call(
         functools.partial(tiles_kernel, first, last),
-        out_shape=jax.ShapeDtypeStruct(total.shape, total.dtype),
-        in_specs=[in_vmem(), in_smem(), in_vmem(), in_vmem(), in_vmem()],
-        out_specs=in_vmem(),
+        out_shape=tuple(shapes),
+        in_specs=specs,
+        out_specs=tuple(in_vmem() for _ in shapes),
         input_output_aliases={4: 0},
+        scratch_shapes=scratch,
         cost_estimate=pl.CostEstimate(
             flops=2 * total.shape[0] * depth * width * (last - first),
             bytes_accessed=0,
@@ -139,7 +157,7 @@
         ),
         compiler_params=pltpu.CompilerParams(vmem_limit_bytes=16 << 20),
         name="tiles",
-    )(table, count, mixed, tiles, total)
+    )(*operands)
 
 
 def far_rows(half, coeff_ref, matrix_ref, near_ref, rows_ref, columns):
@@ -225,7 +243,7 @@
     places = jnp.sum(jnp.where(found, ids[None, :], 0), axis=1)
     table = jnp.stack([places, tile_pairs[:, 1]])
     count = jnp.minimum(tile_count, slots)
-    cut = slots * 3 // 4
+    cut = slots * 2 // 3
 
     first_core = core == 0
     keep, send = partial_call(densities, compress.reshape(points, 2 * rank))
@@ -251,9 +269,9 @@
         if section == 0:
             mixed, near = first_call(densities, clusters)
         elif section == 1:
-            near = tiles_call(0, cut, table, count, mixed, tiles, near)
+            near, held = tiles_call(0, cut, table, count, mixed, tiles, near, expand)
         elif section == 2:
-            near = tiles_call(cut, slots, table, count, mixed, tiles, near)
+            (near,) = tiles_call(cut, slots, table, count, mixed, tiles, near)
         own = jnp.dot(
             paired(coefficients), own_matrices[section], preferred_element_type=jnp.float32
         )
@@ -263,7 +281,7 @@
         )
         coefficients = updated.astype(jnp.bfloat16)
     others = swapped(coefficients, "tgt", 0)
-    matrix = expand.transpose(1, 0, 2).reshape(2 * rank, points)
+    matrix = held.transpose(1, 0, 2).reshape(2 * rank, points)
     result = expand_call(False, cluster_order, coefficients, matrix, near, None)
     return expand_call(True, cluster_order, others, matrix, near, result)
 

time: 30.5 us -> 30.6 us (level)
    unnamed x13 -> x11, local copies, waits for them, and re-layouts: 4.25 us -> 4.24 us
where the time goes in v2:
time: 30.6 us; the launch traced here: 30.4 us
  waiting for transfers between devices  10.5 us (34%)
  Pallas kernels  6.74 us (22%)
  starting transfers between devices  5.28 us (17%)
  local copies, waits for them, and re-layouts  5.18 us (17%)
  matrix products  1.14 us (4%)
  between operations  0.88 us (3%)
  other arithmetic  0.7 us (2%)
    ppermute x7, waiting for transfers between devices, swapped(): return lax.ppermute(value, axis, pairs)  10.5 us
    ppermute x7, starting transfers between devices, swapped(): return lax.ppermute(value, axis, pairs)  5.28 us
    unnamed x11, local copies, waits for them, and re-layouts  4.24 us
    pallas_call x2, Pallas kernels, tiles_call(): pl.pallas_call(functools.partial(tiles_kernel, first, last), out_shape=tu...  2.91 us
    pallas_call x2, Pallas kernels, expand_call(): pl.pallas_call(functools.partial(expand_kernel, flip), out_shape=jax.Shap...  2.29 us
    transpose x1, local copies, waits for them, and re-layouts, shards(): matrix = held.transpose(1, 0, 2).reshape(2 * rank, points)  0.88 us
    pallas_call x1, Pallas kernels, first_call(): pl.pallas_call(first_kernel, out_shape=(jax.ShapeDtypeStruct((clusters, r...  0.81 us
    pallas_call x1, Pallas kernels, partial_call(): pl.pallas_call(partial_kernel, out_shape=(jax.ShapeDtypeStruct((rows // 2...  0.74 us
  transfers between devices with their start and end apart: 7, of which 3 were waited for; matrix products, arithmetic and copies ran while one was open for 16% of the time, Pallas kernels for 18%

profile of v2, /device:TPU:29, one launch (start us, length us, event | category | flops | bytes accessed | tf_op | source)
XLA Modules:
  0.0 30.4 jit_solution(6056537909948008897)
XLA Ops:
  0.0 1.0 %copy.25 = bf16[3,256,2,128]{3,1,2,0:T(8,128)(2,1)S(1)} copy(bf16[3,256,2,128]{3,2,1,0:T(2,128)(2,1)} %param.11) | data formatting | bytes 786432 | tf_op args[2]
  1.1 0.7 %collective-permute-start.2 = (bf16[3,2,256,128]{3,2,1,0:T(8,128)(2,1)S(1)}, bf16[3,2,256,128]{3,2,1,0:T(8,128)(2,1)S(1)}, u32[]{:S(2)}, u32[]{:S(2)}) collective-permute-start(bf16[3,2,256,128]{3,2,1,0:T(8,128)(2,1)S(1)} %bitcast.44), channel_id=1, source_target_pairs={{0,1},{1,0},{2,3},{3,2},{4,5},{5,4},{6,7},{7,6},{8,9},{9,8},{10,11... | collective-permute-start | bytes 1179656 | tf_op jit(solution)/shard_map/ppermute | solution.py:30
  1.8 1.0 %copy.24 = bf16[3,256,2,128]{3,1,2,0:T(8,128)(2,1)S(1)} copy(bf16[3,256,2,128]{3,2,1,0:T(2,128)(2,1)} %param.12) | data formatting | bytes 786432 | tf_op args[3]
  2.8 0.1 collective-permute-start.1
  2.9 2.1 %copy.20 = bf16[256,8,2,256]{3,1,2,0:T(8,128)(2,1)S(1)} copy(bf16[256,8,2,256]{3,2,1,0:T(2,128)(2,1)} %bitcast.41) | data formatting | bytes 4194304
  5.1 0.0 copy-start.3
  5.1 0.0 copy-start.2
  5.1 0.7 %partial.1 = (f32[128,256]{1,0:T(8,128)S(1)}, bf16[128,256]{1,0:T(8,128)(2,1)S(1)}) custom-call(bf16[256,2048]{1,0:T(8,128)(2,1)S(1)} %copy-done.1, bf16[2048,512]{1,0:T(8,128)(2,1)S(1)} %bitcast.38), custom_call_target="tpu_custom_call" | custom-call | flops 536870912 | tf_op jit(solution)/shard_map/partial/pallas_call | solution.py:59
  5.8 0.6 %collective-permute-start = (bf16[128,256]{1,0:T(8,128)(2,1)S(1)}, bf16[128,256]{1,0:T(8,128)(2,1)S(1)}, u32[]{:S(2)}, u32[]{:S(2)}) collective-permute-start(bf16[128,256]{1,0:T(8,128)(2,1)S(1)} %get-tuple-element.14), channel_id=1, source_target_pairs={{0,1},{1,0},{2,3},{3,2},{4,5},{5,4},{6,7},{7,6},{8,9},{9,8},{10,11... | collective-permute-start | bytes 196616 | tf_op jit(solution)/shard_map/ppermute | solution.py:30
  6.4 0.1 select_reduce_fusion
  7.2 0.8 %weave.1 = (bf16[16,256,256]{2,1,0:T(8,128)(2,1)S(1)}, f32[256,2176]{1,0:T(8,128)S(1)}) custom-call(bf16[256,2048]{1,0:T(8,128)(2,1)S(1)} %copy-done.1), custom_call_target="tpu_custom_call" | custom-call | flops 268435456 | tf_op jit(solution)/shard_map/weave/pallas_call | solution.py:118
  8.0 0.3 collective-permute-start.3
  8.3 3.4 %collective-permute-done.3 = bf16[128,256]{1,0:T(8,128)(2,1)S(1)} collective-permute-done((bf16[128,256]{1,0:T(8,128)(2,1)S(1)}, bf16[128,256]{1,0:T(8,128)(2,1)S(1)}, u32[]{:S(2)}, u32[]{:S(2)}) %collective-permute-start.3) | collective-permute-done | bytes 65568 | tf_op jit(solution)/shard_map/ppermute | solution.py:30
  11.7 0.3 maximum_select_fusion
  12.0 0.2 fusion.7
  12.2 0.3 maximum_select_fusion.1
  12.5 0.1 fusion.60
  12.5 0.2 fusion
  12.8 0.2 collective-permute-start.4
  13.0 0.2 fusion.5
  13.2 2.7 %collective-permute-done.4 = bf16[128,256]{1,0:T(8,128)(2,1)S(1)} collective-permute-done((bf16[128,256]{1,0:T(8,128)(2,1)S(1)}, bf16[128,256]{1,0:T(8,128)(2,1)S(1)}, u32[]{:S(2)}, u32[]{:S(2)}) %collective-permute-start.4) | collective-permute-done | bytes 65568 | tf_op jit(solution)/shard_map/ppermute | solution.py:30
  16.0 0.2 fusion.1
  16.2 0.1 collective-permute-start.5
  16.3 0.2 fusion.3
  16.5 4.3 %collective-permute-done.5 = bf16[128,256]{1,0:T(8,128)(2,1)S(1)} collective-permute-done((bf16[128,256]{1,0:T(8,128)(2,1)S(1)}, bf16[128,256]{1,0:T(8,128)(2,1)S(1)}, u32[]{:S(2)}, u32[]{:S(2)}) %collective-permute-start.5) | collective-permute-done | bytes 65568 | tf_op jit(solution)/shard_map/ppermute | solution.py:30
  20.9 0.2 fusion.2.coeff_ref
  21.0 3.3 %collective-permute-start.6 = (bf16[128,256]{1,0:T(8,128)(2,1)S(1)}, bf16[128,256]{1,0:T(8,128)(2,1)S(1)}, u32[]{:S(2)}, u32[]{:S(2)}) collective-permute-start(bf16[128,256]{1,0:T(8,128)(2,1)S(1)} %fusion.2.coeff_ref), channel_id=1, source_target_pairs={{0,1},{1,0},{2,3},{3,2},{4,5},{5,4},{6,7},{7,6},{8,9},{9,8},{10,11... | collective-permute-start | bytes 196616 | tf_op jit(solution)/shard_map/ppermute | solution.py:30
  24.3 1.8 %tiles.2 = (f32[256,2176]{1,0:T(8,128)S(1)}, bf16[256,2,2048]{2,1,0:T(2,128)(2,1)S(1)}) custom-call(s32[2,64]{1,0:T(2,128)S(1)} %pad_add_fusion.table_ref, s32[1]{0:T(128)S(6)} %min.3.count_ref, bf16[16,256,256]{2,1,0:T(8,128)(2,1)S(1)} %get-tuple-element.17.mixed_ref, bf16[64,256,128]{2,1,0:T(8,128)(2,1)S(1)} %bitcast.36, ...), custom_call_target="tpu_custom_call", output_to_operand_aliasing={{0}: (4, {})} | custom-call | flops 704643072 | tf_op jit(solution)/shard_map/tiles/pallas_call | solution.py:146
  26.1 0.9 %copy.19 = bf16[2,256,2048]{2,1,0:T(8,128)(2,1)S(1)} copy(bf16[2,256,2048]{2,0,1:T(2,128)(2,1)S(1)} %bitcast.39) | data formatting | bytes 4194304 | tf_op jit(solution)/shard_map/transpose | solution.py:284
  27.0 1.1 %tiles.3.near_ref = f32[256,2176]{1,0:T(8,128)S(1)} custom-call(s32[2,64]{1,0:T(2,128)S(1)} %pad_add_fusion.table_ref, s32[1]{0:T(128)S(6)} %min.3.count_ref, bf16[16,256,256]{2,1,0:T(8,128)(2,1)S(1)} %get-tuple-element.17.mixed_ref, bf16[64,256,128]{2,1,0:T(8,128)(2,1)S(1)} %bitcast.37, ...), custom_call_target="tpu_custom_call", output_to_operand_aliasing={{}: (4, {})} | custom-call | flops 369098752 | tf_op jit(solution)/shard_map/tiles/pallas_call | solution.py:146
  28.1 1.1 %expand0.1.refs_0_ = bf16[256,2048]{1,0:T(8,128)(2,1)} custom-call(s32[1,16]{1,0:T(1,128)S(1)} %copy-done.2, bf16[128,256]{1,0:T(8,128)(2,1)S(1)} %fusion.2.coeff_ref, bf16[512,2048]{1,0:T(8,128)(2,1)S(1)} %bitcast.34, f32[256,2176]{1,0:T(8,128)S(1)} %tiles.3.near_ref), custom_call_target="tpu_custom_call" | custom-call | flops 268435456 | tf_op jit(solution)/shard_map/expand0/pallas_call | solution.py:212
  29.3 1.1 %expand1.1 = bf16[256,2048]{1,0:T(8,128)(2,1)} custom-call(s32[1,16]{1,0:T(1,128)S(1)} %copy-done.2, bf16[128,256]{1,0:T(8,128)(2,1)S(1)} %collective-permute-done.6.coeff_ref, bf16[512,2048]{1,0:T(8,128)(2,1)S(1)} %bitcast.35, f32[256,2176]{1,0:T(8,128)S(1)} %tiles.3.near_ref, bf16[256,2048]{1,0:T(8,128)(2,1)} %expand0.1.refs_0_), custom_call_target="tpu_custom_call", output_to_operand_aliasing={{}: (4, {})} | custom-call | flops 268435456 | tf_op jit(solution)/shard_map/expand1/pallas_call | solution.py:212
  (19 shorter events, 0.1 us)
Async XLA Ops:
  1.1 10.7 %collective-permute-start.2 = (bf16[3,2,256,128]{3,2,1,0:T(8,128)(2,1)S(1)}, bf16[3,2,256,128]{3,2,1,0:T(8,128)(2,1)S(1)}, u32[]{:S(2)}, u32[]{:S(2)}) collective-permute-start(bf16[3,2,256,128]{3,2,1,0:T(8,128)(2,1)S(1)} %bitcast.44), channel_id=1, source_target_pairs={{0,1},{1,0},{2,3},{3,2},{4,5},{5,4},{6,7},{7,6},{8,9},{9,8},{10,11... | collective-permute-start | bytes 1179656 | tf_op jit(solution)/shard_map/ppermute | solution.py:30
  2.8 9.1 %collective-permute-start.1 = (bf16[3,2,256,128]{3,2,1,0:T(8,128)(2,1)S(1)}, bf16[3,2,256,128]{3,2,1,0:T(8,128)(2,1)S(1)}, u32[]{:S(2)}, u32[]{:S(2)}) collective-permute-start(bf16[3,2,256,128]{3,2,1,0:T(8,128)(2,1)S(1)} %bitcast.42), channel_id=1, source_target_pairs={{0,1},{1,0},{2,3},{3,2},{4,5},{5,4},{6,7},{7,6},{8,9},{9,8},{10,11... | collective-permute-start | bytes 1179656 | tf_op jit(solution)/shard_map/ppermute | solution.py:30
  2.9 2.1 %copy-start.1 = (bf16[256,2048]{1,0:T(8,128)(2,1)S(1)}, bf16[256,2048]{1,0:T(8,128)(2,1)}, u32[]{:S(2)}) copy-start(bf16[256,2048]{1,0:T(8,128)(2,1)} %dens_ref.3) | copy-start | bytes 3145732
  5.1 1.3 %copy-start.3 = (s32[64,2]{0,1:T(2,128)S(1)}, s32[64,2]{0,1:T(2,128)}, u32[]{:S(2)}) copy-start(s32[64,2]{0,1:T(2,128)} %param.15) | copy-start | bytes 1540
  5.1 1.3 %copy-start.2 = (s32[1,16]{1,0:T(1,128)S(1)}, s32[1,16]{1,0:T(1,128)}, u32[]{:S(2)}) copy-start(s32[1,16]{1,0:T(1,128)} %order_ref.3) | copy-start | bytes 196
  5.8 2.1 %collective-permute-start = (bf16[128,256]{1,0:T(8,128)(2,1)S(1)}, bf16[128,256]{1,0:T(8,128)(2,1)S(1)}, u32[]{:S(2)}, u32[]{:S(2)}) collective-permute-start(bf16[128,256]{1,0:T(8,128)(2,1)S(1)} %get-tuple-element.14), channel_id=1, source_target_pairs={{0,1},{1,0},{2,3},{3,2},{4,5},{5,4},{6,7},{7,6},{8,9},{9,8},{10,11... | collective-permute-start | bytes 196616 | tf_op jit(solution)/shard_map/ppermute | solution.py:30
  8.0 3.7 %collective-permute-start.3 = (bf16[128,256]{1,0:T(8,128)(2,1)S(1)}, bf16[128,256]{1,0:T(8,128)(2,1)S(1)}, u32[]{:S(2)}, u32[]{:S(2)}) collective-permute-start(bf16[128,256]{1,0:T(8,128)(2,1)S(1)} %add_convert_fusion), channel_id=1, source_target_pairs={{0,2},{2,0},{4,6},{6,4},{8,10},{10,8},{12,14},{14,12},{1,3},{3,1},... | collective-permute-start | bytes 196616 | tf_op jit(solution)/shard_map/ppermute | solution.py:30
  12.5 11.8 %copy-start = (bf16[64,128,2,128]{3,2,1,0:T(2,128)(2,1)S(1)}, bf16[64,128,2,128]{3,2,1,0:T(2,128)(2,1)}, u32[]{:S(2)}) copy-start(bf16[64,128,2,128]{3,2,1,0:T(2,128)(2,1)} %param.14) | copy-start | bytes 12582916
  12.8 3.2 %collective-permute-start.4 = (bf16[128,256]{1,0:T(8,128)(2,1)S(1)}, bf16[128,256]{1,0:T(8,128)(2,1)S(1)}, u32[]{:S(2)}, u32[]{:S(2)}) collective-permute-start(bf16[128,256]{1,0:T(8,128)(2,1)S(1)} %fusion), channel_id=1, source_target_pairs={{0,4},{2,6},{4,0},{6,2},{8,12},{10,14},{12,8},{14,10},{1,5},{3,7},... | collective-permute-start | bytes 196616 | tf_op jit(solution)/shard_map/ppermute | solution.py:30
  16.2 4.7 %collective-permute-start.5 = (bf16[128,256]{1,0:T(8,128)(2,1)S(1)}, bf16[128,256]{1,0:T(8,128)(2,1)S(1)}, u32[]{:S(2)}, u32[]{:S(2)}) collective-permute-start(bf16[128,256]{1,0:T(8,128)(2,1)S(1)} %fusion.1), channel_id=1, source_target_pairs={{0,8},{2,10},{4,12},{6,14},{8,0},{10,2},{12,4},{14,6},{1,9},{3,11}... | collective-permute-start | bytes 196616 | tf_op jit(solution)/shard_map/ppermute | solution.py:30
  21.0 8.2 %collective-permute-start.6 = (bf16[128,256]{1,0:T(8,128)(2,1)S(1)}, bf16[128,256]{1,0:T(8,128)(2,1)S(1)}, u32[]{:S(2)}, u32[]{:S(2)}) collective-permute-start(bf16[128,256]{1,0:T(8,128)(2,1)S(1)} %fusion.2.coeff_ref), channel_id=1, source_target_pairs={{0,1},{1,0},{2,3},{3,2},{4,5},{5,4},{6,7},{7,6},{8,9},{9,8},{10,11... | collective-permute-start | bytes 196616 | tf_op jit(solution)/shard_map/ppermute | solution.py:30
